TPU v7x, 256 devices: a whole 4x4x8 slice. The times are simulated.
256 devices in a mesh: ctx: 64 (over z_lo, x, y), head: 4 (over z_hi, core).
Axes of the slice: x: 4, y: 4, z: 8 (z_hi: 2, z_lo: 4; z = z_hi * 4 + z_lo), core: 2. Of those that a mesh axis runs over, the one named last changes fastest.
Arguments:
- queries: bfloat16 [65536, 2048], P('ctx', 'head'), may hold values from -18 to 18
- keys: bfloat16 [65536, 2048], P('ctx', 'head'), may hold values from -6 to 6
- values: bfloat16 [65536, 2048], P('ctx', 'head'), may hold values from -6 to 6
- rates: float32 [65536, 4], P('ctx', 'head'), may hold values from 0.00017263349 to 0.0017263349
- fast_w1: bfloat16 [4, 512, 512], P('head'), may hold values from -0.25 to 0.25
- fast_w2: bfloat16 [4, 512, 512], P('head'), may hold values from -2 to 2
- fast_w3: bfloat16 [4, 512, 512], P('head'), may hold values from -0.25 to 0.25
- norm_gain: bfloat16 [2048], P('head'), may hold values from 0.25 to 1.75
- out_weight: bfloat16 [2048, 2048], P('head'), may hold values from -0.125 to 0.125
Outputs:
- output: bfloat16 [65536, 2048], P(('ctx', 'head'))
All inputs are finite; a program needn't handle non-finite values.
Results may differ from a plain program's by a relative error of at most 0.014.
Values may be sent and summed in bfloat16 or wider, within the bound.
A program may use at most 64 MiB of HBM per device.

v0:
```python
import math

import jax
import jax.numpy as jnp
from jax import lax
from jax.sharding import PartitionSpec as P

WINDOW = 256


EPSILON = 1e-06


def from_behind(value, axis, by):
    count = lax.axis_size(axis)
    pairs = [(i, i + by) for i in range(count) if 0 <= i + by < count]
    return lax.ppermute(value, axis, pairs)


def contract_rows(left_side, right_side):
    return lax.dot_general(
        left_side, right_side, (((0,), (0,)), ((), ())), preferred_element_type=jnp.float32
    )


def renorm(weight, push, axis_dim):
    widened = weight.astype(jnp.float32)
    updated = widened + push
    old_norm = jnp.sqrt(jnp.mean(widened * widened, axis=axis_dim, keepdims=True) + EPSILON)
    new_norm = jnp.sqrt(jnp.mean(updated * updated, axis=axis_dim, keepdims=True) + EPSILON)
    return (updated * (old_norm / new_norm)).astype(jnp.bfloat16)


def fast_pushes(key_rows, value_rows, rate_column, gate_weight, down_weight, up_weight):
    gate_part = jnp.dot(key_rows, gate_weight, preferred_element_type=jnp.float32)
    up_part = jnp.dot(key_rows, up_weight, preferred_element_type=jnp.float32)
    sigmoid_gate = jax.nn.sigmoid(gate_part)
    activation = (gate_part * sigmoid_gate * up_part).astype(jnp.bfloat16)
    scaled = (value_rows.astype(jnp.float32) * rate_column).astype(jnp.bfloat16)
    back_grad = lax.dot_general(
        scaled, down_weight, (((1,), (1,)), ((), ())), preferred_element_type=jnp.float32
    )
    grad_gate = (
        back_grad * up_part * sigmoid_gate * (1.0 + gate_part * (1.0 - sigmoid_gate))
    ).astype(jnp.bfloat16)
    grad_up = (back_grad * gate_part * sigmoid_gate).astype(jnp.bfloat16)
    return (
        contract_rows(key_rows, grad_gate),
        contract_rows(activation, scaled),
        contract_rows(key_rows, grad_up),
    )


def apply_fast(query_rows, gate_weight, down_weight, up_weight):
    gate_part = jnp.dot(query_rows, gate_weight, preferred_element_type=jnp.float32)
    up_part = jnp.dot(query_rows, up_weight, preferred_element_type=jnp.float32)
    mixed_act = (gate_part * jax.nn.sigmoid(gate_part) * up_part).astype(jnp.bfloat16)
    return jnp.dot(mixed_act, down_weight, preferred_element_type=jnp.float32)


def window_block(query_block, key_block, value_block, query_first, key_first):
    scores = lax.dot_general(
        query_block, key_block, (((1,), (1,)), ((), ())), preferred_element_type=jnp.float32
    )
    scores = scores * (1.0 / math.sqrt(query_block.shape[1]))
    query_pos = query_first + jnp.arange(query_block.shape[0], dtype=jnp.int32)
    key_pos = key_first + jnp.arange(key_block.shape[0], dtype=jnp.int32)
    allowed = (
        (key_pos[None, :] <= query_pos[:, None])
        & (key_pos[None, :] > query_pos[:, None] - WINDOW)
        & (key_pos[None, :] >= 0)
    )
    scores = jnp.where(allowed, scores, -jnp.inf)
    row_peak = jnp.max(scores, axis=1, keepdims=True)
    exponent = jnp.exp(scores - row_peak)
    weights = (exponent / jnp.sum(exponent, axis=1, keepdims=True)).astype(jnp.bfloat16)
    return jnp.dot(weights, value_block, preferred_element_type=jnp.float32)


def body(queries, keys, values, rates, fast_w1, fast_w2, fast_w3, norm_gain, out_weight):
    tok_rows = queries.shape[0]
    head_width = queries.shape[1]
    stacked = jnp.concatenate([fast_w1, fast_w2, fast_w3], axis=0)
    push_one, push_two, push_three = fast_pushes(
        keys, values, rates, fast_w1[0], fast_w2[0], fast_w3[0]
    )
    pushes = jnp.stack([push_one, push_two, push_three])
    key_tail, value_tail = from_behind(
        (keys[tok_rows - WINDOW :], values[tok_rows - WINDOW :]), "ctx", 1
    )
    summed = lax.psum(pushes, "ctx")
    renewed = renorm(stacked, summed, 1)
    fast_out = apply_fast(queries, renewed[0], renewed[1], renewed[2])
    key_ext = jnp.concatenate([key_tail, keys], axis=0)
    value_ext = jnp.concatenate([value_tail, values], axis=0)
    offset = lax.axis_index("ctx") * tok_rows
    block_rows = min(512, tok_rows)
    pieces = []
    for block_index in range(tok_rows // block_rows):
        first_row = block_index * block_rows
        pieces.append(
            window_block(
                queries[first_row : first_row + block_rows],
                key_ext[first_row : first_row + block_rows + WINDOW],
                value_ext[first_row : first_row + block_rows + WINDOW],
                offset + first_row,
                offset + first_row - WINDOW,
            )
        )
    window_out = jnp.concatenate(pieces, axis=0)
    combined = fast_out + window_out
    heads_count = lax.axis_size("head")
    squares = lax.psum(jnp.sum(combined * combined, axis=1), "head")
    mean_square = (squares / (head_width * heads_count))[:, None]
    normed = (combined * lax.rsqrt(mean_square + EPSILON) * norm_gain.astype(jnp.float32)).astype(
        jnp.bfloat16
    )
    return lax.psum_scatter(
        jnp.dot(normed, out_weight, preferred_element_type=jnp.float32).astype(jnp.bfloat16),
        "head",
        scatter_dimension=0,
        tiled=True,
    )


def solution(mesh):
    placed = (
        P("ctx", "head"),
        P("ctx", "head"),
        P("ctx", "head"),
        P("ctx", "head"),
        P("head", None, None),
        P("head", None, None),
        P("head", None, None),
        P("head"),
        P("head", None),
    )
    return jax.shard_map(
        body, mesh=mesh, in_specs=placed, out_specs=P(("ctx", "head"), None), check_vma=False
    )
```

profile of v0, /device:TPU:5, one launch (start us, length us, event | category | flops | bytes accessed | tf_op | source)
XLA Modules:
  0.0 855.2 jit_solution(4448781565145398050)
XLA Ops:
  6.5 0.0 copy-start
  6.5 2.2 fusion.20
  8.8 0.0 copy-start.8
  8.8 0.0 copy-start.9
  8.8 0.0 copy-start.14
  8.8 0.7 fusion.22
  9.5 0.3 copy-done.8
  9.8 0.3 copy-done.9
  10.2 0.8 fusion.24
  10.9 0.8 convolution_bitcast_fusion
  11.7 1.3 convolution_bitcast_fusion.2
  13.0 1.2 convolution_bitcast_fusion.1
  14.3 2.0 pad_maximum_fusion
  16.3 0.0 all-reduce.2.cloned.1.call-update
  16.3 0.0 copy-start.15
  16.3 0.0 reduce-scatter.2.cloned.1.call-start
  16.4 0.7 slice.36
  17.1 3.2 collective-permute-start
  20.3 1.0 slice.39
  21.3 3.4 collective-permute-start.1
  24.7 2.1 copy.10
  26.8 2.1 copy.11
  28.8 2.0 copy.12
  30.9 0.0 copy-done.15
  31.0 0.0 copy-start.10
  31.0 2.0 fusion.34
  33.0 0.3 fusion.6
  33.2 0.0 copy-start.11
  33.2 1.6 fusion.14
  34.9 0.0 collective-permute-done
  34.9 1.8 fusion.35
  36.6 0.3 fusion.5
  36.9 0.0 collective-permute-done.1
  36.9 2.7 fusion.11
  39.6 640.9 %all-reduce.2.cloned.1.call-done = f32[3,512,512]{1,2,0:T(8,128)} async-done(((f32[3,512,512]{1,2,0:T(8,128)}), f32[3,512,512]{1,2,0:T(8,128)}) %all-reduce.2.cloned.1.call-update) | async-done | bytes 3145744 | tf_op jit(solution)/shard_map/psum | solution.py:91
  680.5 0.0 copy-done.3
  680.5 2.9 fusion
  683.4 0.1 copy-done.1
  683.5 0.1 copy-done.5
  683.6 0.4 multiply_convert_fusion
  684.0 0.0 copy-start.6
  684.0 1.1 copy-done.6
  685.1 2.1 fusion.19
  687.2 5.3 multiply_reduce_fusion.1
  692.5 55.2 %psum.15 = f32[1024]{0:T(1024)S(1)} all-reduce(f32[1024]{0:T(1024)S(1)} %get-tuple-element.11), channel_id=1, replica_groups=mesh['ctx'=64,'head'=4] {'head'}, use_global_device_ids=true, to_apply=%region_8.9 | all-reduce | flops 1024 | bytes 8192 | tf_op jit(solution)/shard_map/psum | solution.py:113
  747.7 6.0 convolution_convert_fusion
  753.7 0.0 reduce-scatter.2.cloned.1.call-update
  753.7 94.6 %reduce-scatter.2.cloned.1.call-done = bf16[256,2048]{1,0:T(8,128)(2,1)} async-done(((bf16[1024,2048]{1,0:T(8,128)(2,1)}), bf16[256,2048]{1,0:T(8,128)(2,1)}) %reduce-scatter.2.cloned.1.call-update) | async-done | bytes 1048592 | tf_op jit(solution)/shard_map/reduce_scatter | solution.py:118
  (27 shorter events, 0.1 us)
Async XLA Ops:
  6.5 741.2 %copy-start = (bf16[512,2048]{1,0:T(8,128)(2,1)S(1)}, bf16[512,2048]{1,0:T(8,128)(2,1)}, u32[]{:S(2)}) copy-start(bf16[512,2048]{1,0:T(8,128)(2,1)} %param.17) | copy-start | bytes 6291460
  6.5 2.2 copy-start.2
  6.5 674.0 %all-reduce.2.cloned.1.call-start = ((), (), s32[]{:S(2)}) async-start(), calls=%async_computation.1 | async-start | bytes 6291456 | tf_op jit(solution)/shard_map/psum | solution.py:91
  6.5 2.2 copy-start.7
  8.8 1.0 copy-start.8
  8.8 1.4 copy-start.9
  8.8 1.4 copy-start.14
  16.3 14.6 %copy-start.15 = (bf16[512]{0:T(512)(128)(2,1)S(1)}, bf16[512]{0:T(512)(128)(2,1)}, u32[]{:S(2)}) copy-start(bf16[512]{0:T(512)(128)(2,1)} %param.16) | copy-start | bytes 3076
  16.3 832.0 %reduce-scatter.2.cloned.1.call-start = ((), (), s32[]{:S(2)}) async-start(), calls=%async_computation.2 | async-start | bytes 5242880 | tf_op jit(solution)/shard_map/reduce_scatter | solution.py:118
  17.1 17.8 %collective-permute-start = (bf16[256,512]{1,0:T(8,128)(2,1)}, bf16[256,512]{1,0:T(8,128)(2,1)}, u32[]{:S(2)}, u32[]{:S(2)}) collective-permute-start(bf16[256,512]{1,0:T(8,128)(2,1)} %slice.36), channel_id=1, source_target_pairs={{0,4},{4,8},{8,12},{12,16},{16,20},{20,24},{24,28},{28,32},{32,36}... | collective-permute-start | bytes 786440 | tf_op jit(solution)/shard_map/ppermute | solution.py:17
  21.3 15.7 %collective-permute-start.1 = (bf16[256,512]{1,0:T(8,128)(2,1)S(1)}, bf16[256,512]{1,0:T(8,128)(2,1)}, u32[]{:S(2)}, u32[]{:S(2)}) collective-permute-start(bf16[256,512]{1,0:T(8,128)(2,1)S(1)} %slice.39), channel_id=1, source_target_pairs={{0,4},{4,8},{8,12},{12,16},{16,20},{20,24},{24,28},{28,32},{32,36}... | collective-permute-start | bytes 786440 | tf_op jit(solution)/shard_map/ppermute | solution.py:17
  31.0 2.3 copy-start.10
  33.2 1.6 copy-start.11
  36.9 643.6 %copy-start.3 = (bf16[1,512,512]{1,2,0:T(8,128)(2,1)S(1)}, bf16[1,512,512]{1,2,0:T(8,128)(2,1)}, u32[]{:S(2)}) copy-start(bf16[1,512,512]{1,2,0:T(8,128)(2,1)} %copy.10) | copy-start | bytes 1572868
  36.9 643.6 %copy-start.4 = (bf16[1,512,512]{1,2,0:T(8,128)(2,1)S(1)}, bf16[1,512,512]{1,2,0:T(8,128)(2,1)}, u32[]{:S(2)}) copy-start(bf16[1,512,512]{1,2,0:T(8,128)(2,1)} %copy.11) | copy-start | bytes 1572868
  680.5 3.0 copy-start.1
  680.5 3.1 copy-start.5
  683.6 1.5 copy-start.12
  684.0 1.1 copy-start.6
  685.1 2.1 copy-start.13
Sparse Core Ops, SparseCore 0:
  16.4 664.0 all-reduce.1
  753.9 94.4 reduce-scatter.1
where the time goes:
time: 856 us; the launch traced here: 855 us
  waiting for transfers between devices  736 us (86%)
  blocking collectives  55.2 us (6%)
  matrix products  28.4 us (3%)
  between operations  13.6 us (2%)
  local copies, waits for them, and re-layouts  9.94 us (1%)
    psum x1, waiting for transfers between devices, body(): summed = lax.psum(pushes, 'ctx')  641 us
    reduce_scatter x1, waiting for transfers between devices, body(): lax.psum_scatter(jnp.dot(normed, out_weight, preferred_element_type=jnp.f...  94.6 us
    psum x1, blocking collectives, body(): squares = lax.psum(jnp.sum(combined * combined, axis=1), 'head')  55.2 us
  transfers between devices with their start and end apart: 4, of which 2 were waited for; matrix products, arithmetic and copies ran while one was open for 2% of the time, Pallas kernels for 0%

commit v1 on v0

v1 whole, which is shorter than its diff:
```python
import math

import jax
import jax.numpy as jnp
from jax import lax
from jax.experimental import pallas as pl
from jax.experimental.pallas import tpu as pltpu
from jax.sharding import PartitionSpec as P

MESH = pl.DeviceIdType.MESH
WINDOW = 256
EPSILON = 1e-06
TOK = 1024
HD = 512
DM = 2048
NEG = -1e30
BF = jnp.bfloat16
F32 = jnp.float32


def dotf(a, b, ca=1, cb=0):
    return lax.dot_general(a, b, (((ca,), (cb,)), ((), ())), preferred_element_type=F32)


def device(zl, x, y, zh, core):
    return (zl * 16 + x * 4 + y, zh * 2 + core)


def aligned(value, by):
    return pl.multiple_of(value, by)


def layer_kernel(
    q_ref, k_ref, v_ref, rate_ref, w1_ref, w2_ref, w3_ref, gain_ref, ow_ref, o_ref,
    kx, vx, qv, w, rb, act, sc, g1, g3, ps, r1, q2, r2, q3, r3, f, asum, win, wo, cs, cr, acc, gains,
    send_sem, recv_sem, local_sem,
):
    c = lax.axis_index("ctx")
    h = lax.axis_index("head")
    zl, x, y = c // 16, (c // 4) % 4, c % 4
    zh, core = h // 2, h % 2

    def at_x(d):
        return device(zl, (x + d) % 4, y, zh, core)

    def at_y(d):
        return device(zl, x, (y + d) % 4, zh, core)

    def at_z(d):
        return device((zl + d) % 4, x, y, zh, core)

    def at_head(other_z, other_core):
        return device(
            zl, x, y, (zh + other_z) % 2, (core + other_core) % 2
        )

    following = ((c + 1) % 64, h)
    previous = ((c + 63) % 64, h)
    mirror = device(3 - zl, x, y, 1 - zh, core)
    used = [0]
    sends = []

    def put(src, dst, to):
        index = used[0]
        used[0] += 1
        copy = pltpu.make_async_remote_copy(
            src_ref=src, dst_ref=dst, send_sem=send_sem.at[index], recv_sem=recv_sem.at[index],
            device_id=to, device_id_type=MESH,
        )
        copy.start()
        sends.append(copy)
        return copy

    local = []

    def fetch(src, dst):
        copy = pltpu.make_async_copy(src, dst, local_sem.at[len(local)])
        copy.start()
        local.append(copy)
        return copy

    first = [
        fetch(k_ref, kx.at[pl.ds(WINDOW, TOK)]),
        fetch(w1_ref, w.at[0]),
        fetch(w3_ref, w.at[2]),
        fetch(v_ref, vx.at[pl.ds(WINDOW, TOK)]),
        fetch(w2_ref, w.at[1]),
    ]
    get_q = fetch(q_ref, qv)
    own_rows = pl.ds(aligned(h * HD, HD), HD)
    get_wo = fetch(ow_ref, wo.at[own_rows])
    get_gain = fetch(gain_ref, gains.at[h])

    barrier = pltpu.get_barrier_semaphore()
    peers = [at_x(d) for d in (1, 2, 3)] + [at_y(d) for d in (1, 2, 3)] + [at_z(d) for d in (1, 2, 3)]
    peers += [at_head(0, 1), at_head(1, 0), at_head(1, 1), following, previous, mirror]
    for peer in peers:
        pl.semaphore_signal(barrier, inc=1, device_id=peer, device_id_type=MESH)
    pl.semaphore_wait(barrier, len(peers))

    halo = [
        put(k_ref.at[pl.ds(TOK - WINDOW, WINDOW)], kx.at[pl.ds(0, WINDOW)], following),
        put(v_ref.at[pl.ds(TOK - WINDOW, WINDOW)], vx.at[pl.ds(0, WINDOW)], following),
    ]
    row_a = aligned(x * 128 + y * 32, 32)
    row_b = aligned(y * 128 + x * 32, 32)
    crossed = [
        put(
            ow_ref.at[pl.ds(row, 32), pl.ds(col, 1024)],
            wo.at[pl.ds(aligned(h * HD + row, 32), 32), pl.ds(col, 1024)],
            mirror,
        )
        for row, col in ((row_a, 0), (row_b, 1024))
    ]
    own_core = [put(ow_ref, wo.at[own_rows], at_head(0, 1))]
    gain_got = [put(gain_ref, gains.at[h], at_head(a, b)) for a, b in ((0, 1), (1, 0), (1, 1))]

    for group in range(8):
        row = jnp.broadcast_to(rate_ref[group : group + 1, :], (128, 128))
        rb[group * 128 : (group + 1) * 128, :] = jnp.transpose(row)
    for copy in first:
        copy.wait()

    def token_block(i, carry):
        rows = pl.ds(aligned(i * 256, 256), 256)
        ext = pl.ds(aligned(i * 256 + WINDOW, 256), 256)
        key_rows = kx[ext, :]
        gate = dotf(key_rows, w[0])
        up = dotf(key_rows, w[2])
        sig = jax.nn.sigmoid(gate)
        gated = gate * sig
        act[rows, :] = (gated * up).astype(BF)
        rate = rb[rows, :]
        scaled = (vx[ext, :].astype(F32) * jnp.concatenate([rate] * 4, axis=1)).astype(BF)
        sc[rows, :] = scaled
        back = dotf(scaled, w[1], 1, 1)
        g1[rows, :] = (back * up * sig * (1.0 + gate * (1.0 - sig))).astype(BF)
        g3[rows, :] = (back * gated).astype(BF)
        return carry

    lax.fori_loop(0, TOK // 256, token_block, 0)

    own_keys = pl.ds(WINDOW, TOK)
    s1 = []
    for m in (1, 0, 2):
        for block in range(4):
            cols = pl.ds(block * 128, 128)
            left = act[:, cols] if m == 1 else kx[own_keys, cols]
            right = (g1, sc, g3)[m][...]
            ps[m, block * 128 : (block + 1) * 128, :] = dotf(left, right, 0, 0).astype(BF)
        got = []
        for d in (1, 2, 3):
            to_x = pl.ds(aligned(((x + d) % 4) * 128, 128), 128)
            to_y = pl.ds(aligned(((y + d) % 4) * 128, 128), 128)
            got.append(put(ps.at[m, to_x, pl.ds(0, 256)], r1.at[0, d - 1, m], at_x(d)))
            got.append(put(ps.at[m, to_y, pl.ds(256, 256)], r1.at[1, d - 1, m], at_y(d)))
        s1.append((m, got))

    def window_block(b):
        queries = qv[b * 256 : (b + 1) * 256, :]
        scores = dotf(queries, kx[b * 256 : b * 256 + 512, :], 1, 1) * (1.0 / math.sqrt(HD))
        qi = lax.broadcasted_iota(jnp.int32, (256, 512), 0)
        ki = lax.broadcasted_iota(jnp.int32, (256, 512), 1)
        allowed = (ki <= qi + WINDOW) & (ki > qi)
        if b == 0:
            allowed = allowed & (ki >= jnp.where(c == 0, WINDOW, 0))
        scores = jnp.where(allowed, scores, NEG)
        peak = jnp.max(scores, axis=1, keepdims=True)
        expo = jnp.where(allowed, jnp.exp(scores - peak), 0.0)
        weights = (expo / jnp.sum(expo, axis=1, keepdims=True)).astype(BF)
        win[b * 256 : (b + 1) * 256, :] = dotf(weights, vx[b * 256 : b * 256 + 512, :])

    get_q.wait()
    for m in range(3):
        wide = w[m].astype(F32)
        asum[m : m + 1, :] = jnp.sum(wide * wide, axis=0, keepdims=True)
    window_block(1)
    window_block(2)
    for copy in halo:
        copy.wait_recv()

    s2 = []
    for turn, (m, got) in enumerate(s1):
        if turn < 2:
            window_block((3, 0)[turn])
        for copy in got:
            copy.wait_recv()
        own_x = pl.ds(aligned(x * 128, 128), 128)
        own_y = pl.ds(aligned(y * 128, 128), 128)
        for half, own in ((0, own_x), (1, own_y)):
            total = ps[m, own, half * 256 : (half + 1) * 256].astype(F32)
            for d in range(3):
                total = total + r1[half, d, m].astype(F32)
            q2[half, m] = total.astype(BF)
        nxt = []
        for d in (1, 2, 3):
            to_y = pl.ds(aligned(((y + d) % 4) * 32, 32), 32)
            to_x = pl.ds(aligned(((x + d) % 4) * 32, 32), 32)
            nxt.append(put(q2.at[0, m, to_y], r2.at[0, d - 1, m], at_y(d)))
            nxt.append(put(q2.at[1, m, to_x], r2.at[1, d - 1, m], at_x(d)))
        s2.append((m, nxt))
    for m, got in s2:
        for copy in got:
            copy.wait_recv()
        own_y = pl.ds(aligned(y * 32, 32), 32)
        own_x = pl.ds(aligned(x * 32, 32), 32)
        for half, own in ((0, own_y), (1, own_x)):
            total = q2[half, m, own, :].astype(F32)
            for d in range(3):
                total = total + r2[half, d, m].astype(F32)
            q3[2 * half, m] = total[:, :128].astype(BF)
            q3[2 * half + 1, m] = total[:, 128:].astype(BF)
    s3 = [put(q3.at[(zl + d) % 4], r3.at[d - 1], at_z(d)) for d in (1, 2, 3)]
    for copy in s3:
        copy.wait_recv()
    flip = zl // 2
    row_z = pl.ds(aligned((1 - flip) * row_a + flip * row_b, 32), 32)
    col_z = pl.ds(aligned(zl * 128, 128), 128)
    for m in range(3):
        total = q3[zl, m].astype(F32)
        for d in range(3):
            total = total + r3[d, m].astype(F32)
        f[m, row_z, col_z] = total.astype(BF)

    mine = f.at[:, row_z, col_z]
    for copy in [put(mine, mine, at_z(d)) for d in (1, 2, 3)]:
        copy.wait_recv()
    part_a = f.at[:, pl.ds(row_a, 32), pl.ds(0, 256)]
    part_b = f.at[:, pl.ds(row_b, 32), pl.ds(256, 256)]
    s5 = []
    for d in (1, 2, 3):
        s5.append(put(part_a, part_a, at_y(d)))
        s5.append(put(part_b, part_b, at_x(d)))
    for copy in s5:
        copy.wait_recv()
    s6 = []
    for m in (0, 2, 1):
        part_a = f.at[m, pl.ds(aligned(x * 128, 128), 128), pl.ds(0, 256)]
        part_b = f.at[m, pl.ds(aligned(y * 128, 128), 128), pl.ds(256, 256)]
        got = []
        for d in (1, 2, 3):
            got.append(put(part_a, part_a, at_x(d)))
            got.append(put(part_b, part_b, at_y(d)))
        s6.append((m, got))

    h_far = (1 - zh) * 2 + core
    base = h_far * HD
    for copy in crossed:
        copy.wait_recv()
    part_a = wo.at[pl.ds(aligned(base + row_a, 32), 32), pl.ds(0, 1024)]
    part_b = wo.at[pl.ds(aligned(base + row_b, 32), 32), pl.ds(1024, 1024)]
    spread = []
    for d in (1, 2, 3):
        spread.append(put(part_a, part_a, at_y(d)))
        spread.append(put(part_b, part_b, at_x(d)))

    for m, got in s6:
        for copy in got:
            copy.wait_recv()
        updated = w[m].astype(F32) + f[m].astype(F32)
        new_mean = jnp.sum(updated * updated, axis=0, keepdims=True) * (1.0 / HD)
        old_mean = asum[m : m + 1, :] * (1.0 / HD)
        ratio = jnp.sqrt(old_mean + EPSILON) / jnp.sqrt(new_mean + EPSILON)
        w[m] = (updated * ratio).astype(BF)

    for copy in spread:
        copy.wait_recv()
    part_a = wo.at[pl.ds(aligned(base + x * 128, 128), 128), pl.ds(0, 1024)]
    part_b = wo.at[pl.ds(aligned(base + y * 128, 128), 128), pl.ds(1024, 1024)]
    spread = []
    for d in (1, 2, 3):
        spread.append(put(part_a, part_a, at_x(d)))
        spread.append(put(part_b, part_b, at_y(d)))

    arrived = []
    for far, other in ((1, 0), (1, 1), (0, 1), (0, 0)):
        target = ((zh + far) % 2) * 2 + (core + other) % 2
        rows = pl.ds(aligned(target * 256, 256), 256)
        queries = qv[rows, :]
        gate = dotf(queries, w[0])
        up = dotf(queries, w[2])
        mixed = (gate * jax.nn.sigmoid(gate) * up).astype(BF)
        combined = (dotf(mixed, w[1]) + win[rows, :]).astype(BF)
        if far or other:
            cs[rows, :] = combined
            arrived.append((far, other, put(cs.at[rows], cr.at[h], at_head(far, other))))
        else:
            cr[h] = combined

    for copy in own_core + gain_got:
        copy.wait_recv()
    get_gain.wait()
    get_wo.wait()

    def project(far, other, fresh, squares):
        source = ((zh + far) % 2) * 2 + (core + other) % 2
        wide = cr[source].astype(F32)
        squares = squares + jnp.sum(wide * wide, axis=1, keepdims=True)
        gained = (wide * gains[source][0:1, :]).astype(BF)
        rows = pl.ds(aligned(source * HD, HD), HD)
        for n in range(4):
            cols = pl.ds(n * 512, 512)
            part = dotf(gained, wo[rows, cols])
            acc[:, cols] = part if fresh else acc[:, cols] + part
        return squares

    squares = project(0, 0, True, jnp.zeros((256, 1), F32))
    arrived[2][2].wait_recv()
    squares = project(0, 1, False, squares)
    for copy in spread:
        copy.wait_recv()
    far_rows = pl.ds(aligned(base, HD), HD)
    shared = put(wo.at[far_rows], wo.at[far_rows], at_head(0, 1))
    arrived[0][2].wait_recv()
    squares = project(1, 0, False, squares)
    arrived[1][2].wait_recv()
    shared.wait_recv()
    squares = project(1, 1, False, squares)
    scale = lax.rsqrt(squares * (1.0 / DM) + EPSILON)
    o_ref[...] = (acc[...] * scale).astype(BF)
    for copy in sends:
        copy.wait_send()


def body(queries, keys, values, rates, fast_w1, fast_w2, fast_w3, norm_gain, out_weight):
    gain = jnp.broadcast_to(norm_gain.astype(F32)[None, :], (8, HD))
    anywhere = pl.BlockSpec(memory_space=pl.ANY)
    vmem = pl.BlockSpec(memory_space=pltpu.VMEM)
    n_copies = 96
    return pl.pallas_call(
        layer_kernel,
        out_shape=jax.ShapeDtypeStruct((TOK // 4, DM), BF),
        in_specs=[anywhere, anywhere, anywhere, vmem, anywhere, anywhere, anywhere, anywhere, anywhere],
        out_specs=vmem,
        scratch_shapes=[
            pltpu.VMEM((WINDOW + TOK, HD), BF),
            pltpu.VMEM((WINDOW + TOK, HD), BF),
            pltpu.VMEM((TOK, HD), BF),
            pltpu.VMEM((3, HD, HD), BF),
            pltpu.VMEM((TOK, 128), F32),
            pltpu.VMEM((TOK, HD), BF),
            pltpu.VMEM((TOK, HD), BF),
            pltpu.VMEM((TOK, HD), BF),
            pltpu.VMEM((TOK, HD), BF),
            pltpu.VMEM((3, HD, HD), BF),
            pltpu.VMEM((2, 3, 3, 128, 256), BF),
            pltpu.VMEM((2, 3, 128, 256), BF),
            pltpu.VMEM((2, 3, 3, 32, 256), BF),
            pltpu.VMEM((4, 3, 32, 128), BF),
            pltpu.VMEM((3, 3, 32, 128), BF),
            pltpu.VMEM((3, HD, HD), BF),
            pltpu.VMEM((8, HD), F32),
            pltpu.VMEM((TOK, HD), F32),
            pltpu.VMEM((DM, DM), BF),
            pltpu.VMEM((TOK, HD), BF),
            pltpu.VMEM((4, 256, HD), BF),
            pltpu.VMEM((256, DM), F32),
            pltpu.VMEM((4, 8, HD), F32),
            pltpu.SemaphoreType.DMA((n_copies,)),
            pltpu.SemaphoreType.DMA((n_copies,)),
            pltpu.SemaphoreType.DMA((8,)),
        ],
        name="layer",
        compiler_params=pltpu.CompilerParams(
            collective_id=0, has_side_effects=True, vmem_limit_bytes=56 << 20
        ),
    )(
        queries, keys, values, rates.reshape(8, 128),
        fast_w1[0], fast_w2[0], fast_w3[0], gain, out_weight,
    )


def solution(mesh):
    placed = (
        P("ctx", "head"),
        P("ctx", "head"),
        P("ctx", "head"),
        P("ctx", "head"),
        P("head", None, None),
        P("head", None, None),
        P("head", None, None),
        P("head"),
        P("head", None),
    )
    return jax.shard_map(
        body, mesh=mesh, in_specs=placed, out_specs=P(("ctx", "head"), None), check_vma=False
    )
```

time: 856 us -> 91.4 us (0.11)
  the two profiles are of different devices: /device:TPU:5 before, /device:TPU:9 now
where the time goes in v1:
time: 91.4 us; the launch traced here: 91.3 us
  Pallas kernels  87.7 us (96%)
  local copies, waits for them, and re-layouts  3.59 us (4%)
    pallas_call x1, Pallas kernels, body(): pl.pallas_call(layer_kernel, out_shape=jax.ShapeDtypeStruct((TOK // 4, DM...  87.7 us
    unnamed x1, local copies, waits for them, and re-layouts  2.3 us

profile of v1, /device:TPU:9, one launch (start us, length us, event | category | flops | bytes accessed | tf_op | source)
XLA Modules:
  0.0 91.3 jit_solution(16319817522988583409)
XLA Ops:
  0.0 1.3 %broadcast_in_dim.2.gain_ref = f32[8,512]{1,0:T(8,128)} broadcast(bf16[512]{0:T(512)(128)(2,1)} %param.16), dimensions={1} | broadcast | bytes 17408 | tf_op jit(solution)/shard_map/broadcast_in_dim | solution.py:326
  1.3 87.7 %layer.1 = bf16[256,2048]{1,0:T(8,128)(2,1)} custom-call(bf16[1024,512]{1,0:T(8,128)(2,1)} %q_ref.1, bf16[1024,512]{1,0:T(8,128)(2,1)} %k_ref.1, bf16[1024,512]{1,0:T(8,128)(2,1)} %v_ref.1, f32[8,128]{1,0:T(8,128)} %bitcast.7, bf16[512,512]{1,0:T(8,128)(2,1)} %bitcast.4, bf16[512,512]{1,0:T(8,128)(2,1)} %bitcast.5, bf16[512,512]{1,0:T(8,128)(2,1)} %bitcast.6, ...), custom_call_target="tpu_custom_call" | custom-call | tf_op jit(solution)/shard_map/layer/pallas_call | solution.py:330
  89.0 2.3 %copy.11 = bf16[256,2048]{1,0:T(8,128)(2,1)} copy(bf16[256,2048]{1,0:T(8,128)(2,1)} %layer.1) | data formatting | bytes 2097152

commit v2 on v1

--- a/solution.py
+++ b/solution.py
@@ -96,24 +96,6 @@
     peers += [at_head(0, 1), at_head(1, 0), at_head(1, 1), following, previous, mirror]
     for peer in peers:
         pl.semaphore_signal(barrier, inc=1, device_id=peer, device_id_type=MESH)
-    pl.semaphore_wait(barrier, len(peers))
-
-    halo = [
-        put(k_ref.at[pl.ds(TOK - WINDOW, WINDOW)], kx.at[pl.ds(0, WINDOW)], following),
-        put(v_ref.at[pl.ds(TOK - WINDOW, WINDOW)], vx.at[pl.ds(0, WINDOW)], following),
-    ]
-    row_a = aligned(x * 128 + y * 32, 32)
-    row_b = aligned(y * 128 + x * 32, 32)
-    crossed = [
-        put(
-            ow_ref.at[pl.ds(row, 32), pl.ds(col, 1024)],
-            wo.at[pl.ds(aligned(h * HD + row, 32), 32), pl.ds(col, 1024)],
-            mirror,
-        )
-        for row, col in ((row_a, 0), (row_b, 1024))
-    ]
-    own_core = [put(ow_ref, wo.at[own_rows], at_head(0, 1))]
-    gain_got = [put(gain_ref, gains.at[h], at_head(a, b)) for a, b in ((0, 1), (1, 0), (1, 1))]
 
     for group in range(8):
         row = jnp.broadcast_to(rate_ref[group : group + 1, :], (128, 128))
@@ -138,23 +120,40 @@
         g3[rows, :] = (back * gated).astype(BF)
         return carry
 
-    lax.fori_loop(0, TOK // 256, token_block, 0)
-
+    lax.fori_loop(0, 1, token_block, 0)
+    pl.semaphore_wait(barrier, len(peers))
+
+    tail = pl.ds(TOK - WINDOW, WINDOW)
+    head = pl.ds(0, WINDOW)
+    halo = [put(k_ref.at[tail], kx.at[head], following)]
+    row_a = aligned(x * 128 + y * 32, 32)
+    row_b = aligned(y * 128 + x * 32, 32)
+    gain_got = [put(gain_ref, gains.at[h], at_head(a, b)) for a, b in ((0, 1), (1, 0), (1, 1))]
+    lax.fori_loop(1, TOK // 256, token_block, 0)
+
+    order = (0, 2, 1)
     own_keys = pl.ds(WINDOW, TOK)
-    s1 = []
-    for m in (1, 0, 2):
+    s1, s2, s3, s4, s5, s6 = {}, {}, {}, {}, {}, {}
+    for m in order:
         for block in range(4):
             cols = pl.ds(block * 128, 128)
             left = act[:, cols] if m == 1 else kx[own_keys, cols]
             right = (g1, sc, g3)[m][...]
             ps[m, block * 128 : (block + 1) * 128, :] = dotf(left, right, 0, 0).astype(BF)
-        got = []
+        s1[m] = []
         for d in (1, 2, 3):
             to_x = pl.ds(aligned(((x + d) % 4) * 128, 128), 128)
             to_y = pl.ds(aligned(((y + d) % 4) * 128, 128), 128)
-            got.append(put(ps.at[m, to_x, pl.ds(0, 256)], r1.at[0, d - 1, m], at_x(d)))
-            got.append(put(ps.at[m, to_y, pl.ds(256, 256)], r1.at[1, d - 1, m], at_y(d)))
-        s1.append((m, got))
+            s1[m].append(put(ps.at[m, to_x, pl.ds(0, 256)], r1.at[0, d - 1, m], at_x(d)))
+            s1[m].append(put(ps.at[m, to_y, pl.ds(256, 256)], r1.at[1, d - 1, m], at_y(d)))
+    crossed = [
+        put(
+            ow_ref.at[pl.ds(row, 32), pl.ds(col, 1024)],
+            wo.at[pl.ds(aligned(h * HD + row, 32), 32), pl.ds(col, 1024)],
+            mirror,
+        )
+        for row, col in ((row_a, 0), (row_b, 1024))
+    ]
 
     def window_block(b):
         queries = qv[b * 256 : (b + 1) * 256, :]
@@ -174,17 +173,13 @@
     for m in range(3):
         wide = w[m].astype(F32)
         asum[m : m + 1, :] = jnp.sum(wide * wide, axis=0, keepdims=True)
-    window_block(1)
-    window_block(2)
-    for copy in halo:
-        copy.wait_recv()
-
-    s2 = []
-    for turn, (m, got) in enumerate(s1):
-        if turn < 2:
-            window_block((3, 0)[turn])
-        for copy in got:
+
+    def all_of(copies):
+        for copy in copies:
             copy.wait_recv()
+
+    def stage_two(m):
+        all_of(s1[m])
         own_x = pl.ds(aligned(x * 128, 128), 128)
         own_y = pl.ds(aligned(y * 128, 128), 128)
         for half, own in ((0, own_x), (1, own_y)):
@@ -192,16 +187,15 @@
             for d in range(3):
                 total = total + r1[half, d, m].astype(F32)
             q2[half, m] = total.astype(BF)
-        nxt = []
+        s2[m] = []
         for d in (1, 2, 3):
             to_y = pl.ds(aligned(((y + d) % 4) * 32, 32), 32)
             to_x = pl.ds(aligned(((x + d) % 4) * 32, 32), 32)
-            nxt.append(put(q2.at[0, m, to_y], r2.at[0, d - 1, m], at_y(d)))
-            nxt.append(put(q2.at[1, m, to_x], r2.at[1, d - 1, m], at_x(d)))
-        s2.append((m, nxt))
-    for m, got in s2:
-        for copy in got:
-            copy.wait_recv()
+            s2[m].append(put(q2.at[0, m, to_y], r2.at[0, d - 1, m], at_y(d)))
+            s2[m].append(put(q2.at[1, m, to_x], r2.at[1, d - 1, m], at_x(d)))
+
+    def stage_three(m):
+        all_of(s2[m])
         own_y = pl.ds(aligned(y * 32, 32), 32)
         own_x = pl.ds(aligned(x * 32, 32), 32)
         for half, own in ((0, own_y), (1, own_x)):
@@ -210,68 +204,88 @@
                 total = total + r2[half, d, m].astype(F32)
             q3[2 * half, m] = total[:, :128].astype(BF)
             q3[2 * half + 1, m] = total[:, 128:].astype(BF)
-    s3 = [put(q3.at[(zl + d) % 4], r3.at[d - 1], at_z(d)) for d in (1, 2, 3)]
-    for copy in s3:
-        copy.wait_recv()
+        s3[m] = [put(q3.at[(zl + d) % 4, m], r3.at[d - 1, m], at_z(d)) for d in (1, 2, 3)]
+
     flip = zl // 2
     row_z = pl.ds(aligned((1 - flip) * row_a + flip * row_b, 32), 32)
     col_z = pl.ds(aligned(zl * 128, 128), 128)
-    for m in range(3):
+
+    def stage_four(m):
+        all_of(s3[m])
         total = q3[zl, m].astype(F32)
         for d in range(3):
             total = total + r3[d, m].astype(F32)
         f[m, row_z, col_z] = total.astype(BF)
-
-    mine = f.at[:, row_z, col_z]
-    for copy in [put(mine, mine, at_z(d)) for d in (1, 2, 3)]:
-        copy.wait_recv()
-    part_a = f.at[:, pl.ds(row_a, 32), pl.ds(0, 256)]
-    part_b = f.at[:, pl.ds(row_b, 32), pl.ds(256, 256)]
-    s5 = []
-    for d in (1, 2, 3):
-        s5.append(put(part_a, part_a, at_y(d)))
-        s5.append(put(part_b, part_b, at_x(d)))
-    for copy in s5:
-        copy.wait_recv()
-    s6 = []
-    for m in (0, 2, 1):
+        mine = f.at[m, row_z, col_z]
+        s4[m] = [put(mine, mine, at_z(d)) for d in (1, 2, 3)]
+
+    def stage_five(m):
+        all_of(s4[m])
+        part_a = f.at[m, pl.ds(row_a, 32), pl.ds(0, 256)]
+        part_b = f.at[m, pl.ds(row_b, 32), pl.ds(256, 256)]
+        s5[m] = []
+        for d in (1, 2, 3):
+            s5[m].append(put(part_a, part_a, at_y(d)))
+            s5[m].append(put(part_b, part_b, at_x(d)))
+
+    def stage_six(m):
+        all_of(s5[m])
         part_a = f.at[m, pl.ds(aligned(x * 128, 128), 128), pl.ds(0, 256)]
         part_b = f.at[m, pl.ds(aligned(y * 128, 128), 128), pl.ds(256, 256)]
-        got = []
+        s6[m] = []
         for d in (1, 2, 3):
-            got.append(put(part_a, part_a, at_x(d)))
-            got.append(put(part_b, part_b, at_y(d)))
-        s6.append((m, got))
-
-    h_far = (1 - zh) * 2 + core
-    base = h_far * HD
-    for copy in crossed:
-        copy.wait_recv()
+            s6[m].append(put(part_a, part_a, at_x(d)))
+            s6[m].append(put(part_b, part_b, at_y(d)))
+
+    def renew(m):
+        all_of(s6[m])
+        updated = w[m].astype(F32) + f[m].astype(F32)
+        new_mean = jnp.sum(updated * updated, axis=0, keepdims=True) * (1.0 / HD)
+        old_mean = asum[m : m + 1, :] * (1.0 / HD)
+        ratio = jnp.sqrt(old_mean + EPSILON) / jnp.sqrt(new_mean + EPSILON)
+        w[m] = (updated * ratio).astype(BF)
+
+    window_block(1)
+    window_block(2)
+    stage_two(order[0])
+    window_block(3)
+    stage_two(order[1])
+    stage_two(order[2])
+    halo.append(put(v_ref.at[pl.ds(TOK - WINDOW + 0, 64)], vx.at[pl.ds(0, 64)], following))
+    stage_three(order[0])
+    stage_three(order[1])
+    stage_three(order[2])
+    halo.append(put(v_ref.at[pl.ds(TOK - WINDOW + 64, 64)], vx.at[pl.ds(64, 64)], following))
+    halo.append(put(v_ref.at[pl.ds(TOK - WINDOW + 128, 64)], vx.at[pl.ds(128, 64)], following))
+    base = ((1 - zh) * 2 + core) * HD
+    for m in order:
+        stage_four(m)
+    halo.append(put(v_ref.at[pl.ds(TOK - WINDOW + 192, 64)], vx.at[pl.ds(192, 64)], following))
+    for m in order:
+        stage_five(m)
+    for m in order:
+        stage_six(m)
+    all_of(crossed)
     part_a = wo.at[pl.ds(aligned(base + row_a, 32), 32), pl.ds(0, 1024)]
     part_b = wo.at[pl.ds(aligned(base + row_b, 32), 32), pl.ds(1024, 1024)]
     spread = []
     for d in (1, 2, 3):
         spread.append(put(part_a, part_a, at_y(d)))
         spread.append(put(part_b, part_b, at_x(d)))
-
-    for m, got in s6:
-        for copy in got:
-            copy.wait_recv()
-        updated = w[m].astype(F32) + f[m].astype(F32)
-        new_mean = jnp.sum(updated * updated, axis=0, keepdims=True) * (1.0 / HD)
-        old_mean = asum[m : m + 1, :] * (1.0 / HD)
-        ratio = jnp.sqrt(old_mean + EPSILON) / jnp.sqrt(new_mean + EPSILON)
-        w[m] = (updated * ratio).astype(BF)
-
-    for copy in spread:
-        copy.wait_recv()
+    own_core = [put(ow_ref, wo.at[own_rows], at_head(0, 1))]
+    renew(0)
+    all_of(spread)
     part_a = wo.at[pl.ds(aligned(base + x * 128, 128), 128), pl.ds(0, 1024)]
     part_b = wo.at[pl.ds(aligned(base + y * 128, 128), 128), pl.ds(1024, 1024)]
+    renew(2)
+    renew(1)
     spread = []
     for d in (1, 2, 3):
         spread.append(put(part_a, part_a, at_x(d)))
         spread.append(put(part_b, part_b, at_y(d)))
 
+    all_of(halo)
+    window_block(0)
     arrived = []
     for far, other in ((1, 0), (1, 1), (0, 1), (0, 0)):
         target = ((zh + far) % 2) * 2 + (core + other) % 2
@@ -295,8 +309,10 @@
     def project(far, other, fresh, squares):
         source = ((zh + far) % 2) * 2 + (core + other) % 2
         wide = cr[source].astype(F32)
+        gain = gains[source].astype(F32)
+        gain_row = jnp.concatenate([gain[i : i + 1, :] for i in range(4)], axis=1)
         squares = squares + jnp.sum(wide * wide, axis=1, keepdims=True)
-        gained = (wide * gains[source][0:1, :]).astype(BF)
+        gained = (wide * gain_row).astype(BF)
         rows = pl.ds(aligned(source * HD, HD), HD)
         for n in range(4):
             cols = pl.ds(n * 512, 512)
@@ -323,10 +339,9 @@
 
 
 def body(queries, keys, values, rates, fast_w1, fast_w2, fast_w3, norm_gain, out_weight):
-    gain = jnp.broadcast_to(norm_gain.astype(F32)[None, :], (8, HD))
     anywhere = pl.BlockSpec(memory_space=pl.ANY)
     vmem = pl.BlockSpec(memory_space=pltpu.VMEM)
-    n_copies = 96
+    n_copies = 128
     return pl.pallas_call(
         layer_kernel,
         out_shape=jax.ShapeDtypeStruct((TOK // 4, DM), BF),
@@ -355,18 +370,18 @@
             pltpu.VMEM((TOK, HD), BF),
             pltpu.VMEM((4, 256, HD), BF),
             pltpu.VMEM((256, DM), F32),
-            pltpu.VMEM((4, 8, HD), F32),
+            pltpu.VMEM((4, 4, 128), BF),
             pltpu.SemaphoreType.DMA((n_copies,)),
             pltpu.SemaphoreType.DMA((n_copies,)),
             pltpu.SemaphoreType.DMA((8,)),
         ],
         name="layer",
         compiler_params=pltpu.CompilerParams(
-            collective_id=0, has_side_effects=True, vmem_limit_bytes=56 << 20
+            collective_id=0, has_side_effects=True, vmem_limit_bytes=60 << 20
         ),
     )(
         queries, keys, values, rates.reshape(8, 128),
-        fast_w1[0], fast_w2[0], fast_w3[0], gain, out_weight,
+        fast_w1[0], fast_w2[0], fast_w3[0], norm_gain.reshape(4, 128), out_weight,
     )
 
 

time: 91.4 us -> 88.3 us (0.966)
  the two profiles are of different devices: /device:TPU:9 before, /device:TPU:1 now
where the time goes in v2:
time: 88.3 us; the launch traced here: 88.1 us
  Pallas kernels  85.8 us (97%)
  local copies, waits for them, and re-layouts  2.3 us (3%)
    pallas_call x1, Pallas kernels, body(): pl.pallas_call(layer_kernel, out_shape=jax.ShapeDtypeStruct((TOK // 4, DM...  85.8 us
    unnamed x1, local copies, waits for them, and re-layouts  2.3 us

profile of v2, /device:TPU:1, one launch (start us, length us, event | category | flops | bytes accessed | tf_op | source)
XLA Modules:
  0.0 88.1 jit_solution(12527561088028975341)
XLA Ops:
  0.0 85.8 %layer.1 = bf16[256,2048]{1,0:T(8,128)(2,1)} custom-call(bf16[1024,512]{1,0:T(8,128)(2,1)} %q_ref.1, bf16[1024,512]{1,0:T(8,128)(2,1)} %k_ref.1, bf16[1024,512]{1,0:T(8,128)(2,1)} %v_ref.1, f32[8,128]{1,0:T(8,128)} %bitcast.8, bf16[512,512]{1,0:T(8,128)(2,1)} %bitcast.5, bf16[512,512]{1,0:T(8,128)(2,1)} %bitcast.6, bf16[512,512]{1,0:T(8,128)(2,1)} %bitcast.7, ...), custom_call_target="tpu_custom_call" | custom-call | tf_op jit(solution)/shard_map/layer/pallas_call | solution.py:345
  85.8 2.3 %copy.11 = bf16[256,2048]{1,0:T(8,128)(2,1)} copy(bf16[256,2048]{1,0:T(8,128)(2,1)} %layer.1) | data formatting | bytes 2097152

commit v3 on v2

--- a/solution.py
+++ b/solution.py
@@ -86,10 +86,7 @@
         fetch(v_ref, vx.at[pl.ds(WINDOW, TOK)]),
         fetch(w2_ref, w.at[1]),
     ]
-    get_q = fetch(q_ref, qv)
     own_rows = pl.ds(aligned(h * HD, HD), HD)
-    get_wo = fetch(ow_ref, wo.at[own_rows])
-    get_gain = fetch(gain_ref, gains.at[h])
 
     barrier = pltpu.get_barrier_semaphore()
     peers = [at_x(d) for d in (1, 2, 3)] + [at_y(d) for d in (1, 2, 3)] + [at_z(d) for d in (1, 2, 3)]
@@ -97,6 +94,14 @@
     for peer in peers:
         pl.semaphore_signal(barrier, inc=1, device_id=peer, device_id_type=MESH)
 
+    pl.semaphore_wait(barrier, len(peers))
+
+    tail = pl.ds(TOK - WINDOW, WINDOW)
+    head = pl.ds(0, WINDOW)
+    halo = [put(k_ref.at[tail], kx.at[head], following)]
+    row_a = aligned(x * 128 + y * 32, 32)
+    row_b = aligned(y * 128 + x * 32, 32)
+    gain_got = [put(gain_ref, gains.at[h], at_head(a, b)) for a, b in ((0, 1), (1, 0), (1, 1))]
     for group in range(8):
         row = jnp.broadcast_to(rate_ref[group : group + 1, :], (128, 128))
         rb[group * 128 : (group + 1) * 128, :] = jnp.transpose(row)
@@ -120,16 +125,10 @@
         g3[rows, :] = (back * gated).astype(BF)
         return carry
 
-    lax.fori_loop(0, 1, token_block, 0)
-    pl.semaphore_wait(barrier, len(peers))
-
-    tail = pl.ds(TOK - WINDOW, WINDOW)
-    head = pl.ds(0, WINDOW)
-    halo = [put(k_ref.at[tail], kx.at[head], following)]
-    row_a = aligned(x * 128 + y * 32, 32)
-    row_b = aligned(y * 128 + x * 32, 32)
-    gain_got = [put(gain_ref, gains.at[h], at_head(a, b)) for a, b in ((0, 1), (1, 0), (1, 1))]
-    lax.fori_loop(1, TOK // 256, token_block, 0)
+    lax.fori_loop(0, TOK // 256, token_block, 0)
+    get_q = fetch(q_ref, qv)
+    get_wo = fetch(ow_ref, wo.at[own_rows])
+    get_gain = fetch(gain_ref, gains.at[h])
 
     order = (0, 2, 1)
     own_keys = pl.ds(WINDOW, TOK)

time: 88.3 us -> 85.7 us (0.971)
  the two profiles are of different devices: /device:TPU:1 before, /device:TPU:5 now
where the time goes in v3:
time: 85.7 us; the launch traced here: 85.6 us
  Pallas kernels  83.3 us (97%)
  local copies, waits for them, and re-layouts  2.3 us (3%)
    pallas_call x1, Pallas kernels, body(): pl.pallas_call(layer_kernel, out_shape=jax.ShapeDtypeStruct((TOK // 4, DM...  83.3 us
    unnamed x1, local copies, waits for them, and re-layouts  2.3 us

profile of v3, /device:TPU:5, one launch (start us, length us, event | category | flops | bytes accessed | tf_op | source)
XLA Modules:
  0.0 85.6 jit_solution(13803051554601448907)
XLA Ops:
  0.0 83.3 %layer.1 = bf16[256,2048]{1,0:T(8,128)(2,1)} custom-call(bf16[1024,512]{1,0:T(8,128)(2,1)} %q_ref.1, bf16[1024,512]{1,0:T(8,128)(2,1)} %k_ref.1, bf16[1024,512]{1,0:T(8,128)(2,1)} %v_ref.1, f32[8,128]{1,0:T(8,128)} %bitcast.8, bf16[512,512]{1,0:T(8,128)(2,1)} %bitcast.5, bf16[512,512]{1,0:T(8,128)(2,1)} %bitcast.6, bf16[512,512]{1,0:T(8,128)(2,1)} %bitcast.7, ...), custom_call_target="tpu_custom_call" | custom-call | tf_op jit(solution)/shard_map/layer/pallas_call | solution.py:344
  83.3 2.3 %copy.11 = bf16[256,2048]{1,0:T(8,128)(2,1)} copy(bf16[256,2048]{1,0:T(8,128)(2,1)} %layer.1) | data formatting | bytes 2097152

commit v4 on v3

--- a/solution.py
+++ b/solution.py
@@ -271,7 +271,6 @@
     for d in (1, 2, 3):
         spread.append(put(part_a, part_a, at_y(d)))
         spread.append(put(part_b, part_b, at_x(d)))
-    own_core = [put(ow_ref, wo.at[own_rows], at_head(0, 1))]
     renew(0)
     all_of(spread)
     part_a = wo.at[pl.ds(aligned(base + x * 128, 128), 128), pl.ds(0, 1024)]
@@ -300,6 +299,7 @@
         else:
             cr[h] = combined
 
+    own_core = [put(ow_ref, wo.at[own_rows], at_head(0, 1))]
     for copy in own_core + gain_got:
         copy.wait_recv()
     get_gain.wait()

time: 85.7 us -> 85.7 us (level)
  no operation moved by 1% of the time
where the time goes in v4:
time: 85.7 us; the launch traced here: 85.6 us
  Pallas kernels  83.3 us (97%)
  local copies, waits for them, and re-layouts  2.3 us (3%)
    pallas_call x1, Pallas kernels, body(): pl.pallas_call(layer_kernel, out_shape=jax.ShapeDtypeStruct((TOK // 4, DM...  83.3 us
    unnamed x1, local copies, waits for them, and re-layouts  2.3 us

profile of v4, /device:TPU:5, one launch (start us, length us, event | category | flops | bytes accessed | tf_op | source)
XLA Modules:
  0.0 85.6 jit_solution(2368289164164452012)
XLA Ops:
  0.0 83.3 %layer.1 = bf16[256,2048]{1,0:T(8,128)(2,1)} custom-call(bf16[1024,512]{1,0:T(8,128)(2,1)} %q_ref.1, bf16[1024,512]{1,0:T(8,128)(2,1)} %k_ref.1, bf16[1024,512]{1,0:T(8,128)(2,1)} %v_ref.1, f32[8,128]{1,0:T(8,128)} %bitcast.8, bf16[512,512]{1,0:T(8,128)(2,1)} %bitcast.5, bf16[512,512]{1,0:T(8,128)(2,1)} %bitcast.6, bf16[512,512]{1,0:T(8,128)(2,1)} %bitcast.7, ...), custom_call_target="tpu_custom_call" | custom-call | tf_op jit(solution)/shard_map/layer/pallas_call | solution.py:344
  83.3 2.3 %copy.11 = bf16[256,2048]{1,0:T(8,128)(2,1)} copy(bf16[256,2048]{1,0:T(8,128)(2,1)} %layer.1) | data formatting | bytes 2097152
